TPU v7x, 256 devices: a whole 4x4x8 slice. The times are simulated.
256 devices in a mesh: blk: 32 (over x, z), leaf: 4 (over y), samp: 2 (over core).
Axes of the slice: x: 4, y: 4, z: 8, core: 2. Of those that a mesh axis runs over, the one named last changes fastest.
Arguments:
- points: float32 [3, 32768], P(None, ('blk', 'leaf')), may hold values from 0 to 64, as said below
- neighbors: int32 [128, 8], P(('blk', 'leaf')), may hold values from -1 to 127, as said below
- omega: float32 [512, 32768], P(None, ('blk', 'leaf')), may hold values from -6 to 6
- observed: float32 [32768], P(('blk', 'leaf')), may hold values from -6 to 6
- prior_draws: float32 [64, 32768], P('samp', ('blk', 'leaf')), may hold values from -6 to 6
Outputs:
- weights: float32 [64, 32768], P('samp', ('blk', 'leaf'))
- residual: float32 [64, 32768], P('samp', ('blk', 'leaf'))
Inputs may be any that keep to these rules, and one draw needn't show every extreme that they name: Block g's points lie in the unit cell with integer corner (cx, cy, cz), where cx // 2 = g // 4 and 0 <= cy, cz < 3. `neighbors`: row g lists in ascending order every block h whose unit cell touches g's (cells at most one apart in every coordinate, the first taken periodic of period 2 * 32), which includes every block with a point within distance 1 of a point of g, followed by -1 in the unused slots; the relation is symmetric, and every listed block has a slab index h // 4 equal to or cyclically next to g // 4.
All inputs are finite; a program needn't handle non-finite values.
Results may differ from a plain program's by a relative error of at most 0.0003.
Values sent between devices are 32-bit elements; how exact they have to be, the bound alone decides.
A program may use at most 64 MiB of HBM per device.

v0:
```python
import jax
import jax.numpy as jnp
from jax import lax
from jax.sharding import PartitionSpec as P

PB = 256
ITERS = 2
support_radius = 0.8
noise_variance = 1.0
sketch_shift = 1.0
ALL_AXES = ("blk", "leaf", "samp")


def shifted_2(block, axis, distance):
    devices = range(lax.axis_size(axis))
    route = [((i - distance) % len(devices), i) for i in devices]
    return lax.ppermute(block, axis, route)


def wendland(row_points, column_points, period):
    offset = row_points[None, :, :, None] - column_points[:, :, None, :]
    half_period = 0.5 * period
    along_x = jnp.mod(offset[:, 0] + half_period, period) - half_period
    squared = along_x * along_x + offset[:, 1] * offset[:, 1] + offset[:, 2] * offset[:, 2]
    radius = jnp.sqrt(squared) / support_radius
    remain = jnp.maximum(1.0 - radius, 0.0)
    return remain**4 * (4.0 * radius + 1.0)


def high_dot(left, right):
    return jnp.dot(left, right, precision=lax.Precision.HIGHEST, preferred_element_type=jnp.float32)


def shifted(values, offset_by):
    return shifted_2(values, "blk", offset_by)


def beside_all(values):
    slab_values = lax.all_gather(values, "leaf", axis=1, tiled=True)
    return jnp.concatenate([shifted(slab_values, 1), slab_values, shifted(slab_values, -1)], axis=1)


def lower_solve(factor, values):
    return lax.linalg.triangular_solve(factor, values, left_side=True, lower=True)


def local(points, neighbors, omega, observed, prior_draws):
    blk_dev = neighbors.shape[0]
    cycle_count = lax.axis_size("blk")
    slab_blocks = blk_dev * lax.axis_size("leaf")
    period = 2.0 * cycle_count
    own_slab = lax.axis_index("blk")
    n_samp = lax.axis_size("samp")
    samp_idx = lax.axis_index("samp")
    usable = neighbors >= 0
    relative = jnp.mod(neighbors // slab_blocks - own_slab + 1, cycle_count)
    chosen = jnp.where(usable, relative * slab_blocks + jnp.mod(neighbors, slab_blocks), 0)
    usable_weight = usable.astype(jnp.float32)
    reach_points = beside_all(points)
    reach_blocks = reach_points.reshape(3, 3 * slab_blocks, PB).transpose(1, 0, 2)
    row_blocks = points.reshape(3, blk_dev, PB).transpose(1, 0, 2)
    kernel_tile = wendland(row_blocks[0], reach_blocks[chosen[0]], period)
    kernel_tile = kernel_tile * usable_weight[0][:, None, None]

    def apply_kernel(values):
        width = values.shape[0]
        reach = beside_all(values).reshape(width, 3 * slab_blocks, PB)
        picked = jnp.take(reach, chosen[0], axis=1)
        return jnp.einsum("cnj,nij->ci", picked, kernel_tile, precision=lax.Precision.HIGHEST)

    def slot(x):
        zeros = jnp.zeros((n_samp,) + x.shape, x.dtype)
        return lax.dynamic_update_index_in_dim(zeros, x, samp_idx, 0)

    def unslot(xs):
        return lax.dynamic_index_in_dim(xs, samp_idx, 0, keepdims=False)

    def total_per_samp(values):
        return jax.tree.map(unslot, lax.psum(jax.tree.map(slot, values), ALL_AXES))

    sketch = apply_kernel(omega) + sketch_shift * omega
    rhs = observed[None, :] - prior_draws
    half = PB // n_samp
    omega_half = lax.dynamic_slice_in_dim(omega, samp_idx * half, half, axis=1)
    sketch_half = lax.dynamic_slice_in_dim(sketch, samp_idx * half, half, axis=1)
    core_part = high_dot(omega_half, sketch_half.T)
    square_part = high_dot(sketch_half, sketch_half.T)
    rhs_part = slot(high_dot(sketch, rhs.T))
    core_gram, square_gram, rhs_proj = lax.psum((core_part, square_part, rhs_part), ALL_AXES)
    rhs_proj = unslot(rhs_proj)
    core_gram = 0.5 * (core_gram + core_gram.T)
    factor = jnp.linalg.cholesky(core_gram)
    basis = lower_solve(factor, sketch)
    half_solved = lower_solve(factor, square_gram)
    basis_gram = lower_solve(factor, half_solved.T)
    woodbury = noise_variance * jnp.eye(basis.shape[0], dtype=jnp.float32) + 0.5 * (
        basis_gram + basis_gram.T
    )
    wood_factor = jnp.linalg.cholesky(woodbury)

    def precond_from(vectors, projected):
        first_solve = lower_solve(wood_factor, projected)
        solved = lax.linalg.triangular_solve(
            wood_factor, first_solve, left_side=True, lower=True, transpose_a=True
        )
        return (vectors - high_dot(solved.T, basis)) / noise_variance

    residual = rhs
    projected = lower_solve(factor, rhs_proj)
    precond = precond_from(residual, projected)
    direction = precond
    weights = jnp.zeros_like(rhs)
    image = apply_kernel(direction) + noise_variance * direction
    inner_now, curvature, image_proj = total_per_samp(
        (
            jnp.sum(residual * precond, axis=1),
            jnp.sum(direction * image, axis=1),
            high_dot(basis, image.T),
        )
    )
    step_size = inner_now / curvature
    weights = weights + step_size[:, None] * direction
    residual = residual - step_size[:, None] * image
    projected = projected - step_size[None, :] * image_proj
    precond = precond_from(residual, projected)
    inner_next = total_per_samp(jnp.sum(residual * precond, axis=1))
    direction = precond + (inner_next / inner_now)[:, None] * direction
    inner_now = inner_next
    image = apply_kernel(direction) + noise_variance * direction
    curvature = total_per_samp(jnp.sum(direction * image, axis=1))
    step_size = inner_now / curvature
    weights = weights + step_size[:, None] * direction
    residual = residual - step_size[:, None] * image
    return (weights, residual)


def solution(mesh):
    in_specs = (
        P(None, ("blk", "leaf")),
        P(("blk", "leaf"), None),
        P(None, ("blk", "leaf")),
        P(("blk", "leaf")),
        P("samp", ("blk", "leaf")),
    )
    out_specs = (P("samp", ("blk", "leaf")), P("samp", ("blk", "leaf")))
    return jax.shard_map(local, mesh=mesh, in_specs=in_specs, out_specs=out_specs, check_vma=False)
```

profile of v0, /device:TPU:1, one launch (start us, length us, event | category | flops | bytes accessed | tf_op | source)
XLA Modules:
  0.0 1166.5 jit_solution(11193395616657118959)
XLA Ops:
  9.3 10.5 all_gather.13
  19.8 7.8 collective-permute-start.3
  27.6 19.4 %all-gather.2.cloned.1.call-done = f32[512,1024]{0,1:T(8,128)} async-done(((f32[512,256]{0,1:T(8,128)}), f32[512,1024]{0,1:T(8,128)}) %all-gather.2.cloned.1.call-update) | async-done | bytes 2097168 | tf_op jit(solution)/shard_map/all_gather | solution.py:39
  47.1 5.2 collective-permute-start.1
  56.0 2.6 multiply_multiply_fusion
  58.7 38.2 %collective-permute-done.1 = f32[512,1024]{0,1:T(8,128)} collective-permute-done((f32[512,1024]{0,1:T(8,128)}, f32[512,1024]{0,1:T(8,128)}, u32[]{:S(2)}, u32[]{:S(2)}) %collective-permute-start.1) | collective-permute-done | bytes 2097184 | tf_op jit(solution)/shard_map/ppermute | solution.py:17
  96.8 5.2 collective-permute-done
  102.0 5.6 pad_maximum_fusion
  107.6 6.5 copy.12
  114.2 5.6 gather_fusion
  119.8 5.5 fusion.17
  130.8 254.7 %all-reduce.8.cloned.1.call-done = (f32[512,512]{1,0:T(8,128)}, f32[2,512,32]{1,2,0:T(8,128)}, f32[512,512]{1,0:T(8,128)}) async-done(((f32[512,512]{1,0:T(8,128)}, f32[2,512,32]{1,2,0:T(8,128)}, f32[512,512]{1,0:T(8,128)}), (f32[512,512]{1,0:T(8,128)}, f32[2,512,32]{1,2,0:T(8,128)}, f32[512,512]{1,0:T(8,128)})) %all-reduce.8.cloned.1.call-update) | async-done | bytes 2228240 | tf_op jit(solution)/shard_map/psum | solution.py:89
  386.4 2.5 copy.14
  394.6 11.7 %cholesky.286 = f32[128,128]{1,0:T(8,128)S(1)} custom-call(f32[128,128]{1,0:T(8,128)S(1)} %cholesky.426), custom_call_target="Cholesky" | custom-call | tf_op jit(solution)/shard_map/jit(cholesky)/cholesky | solution.py:92
  406.3 9.8 custom-call.40
  418.8 11.7 %cholesky.305 = f32[128,128]{1,0:T(8,128)S(1)} custom-call(f32[128,128]{1,0:T(8,128)S(1)} %cholesky.430), custom_call_target="Cholesky" | custom-call | tf_op jit(solution)/shard_map/jit(cholesky)/cholesky | solution.py:92
  430.5 10.3 custom-call.41
  443.4 11.7 %cholesky.326 = f32[128,128]{1,0:T(8,128)S(1)} custom-call(f32[128,128]{1,0:T(8,128)S(1)} %cholesky.435), custom_call_target="Cholesky" | custom-call | tf_op jit(solution)/shard_map/jit(cholesky)/cholesky | solution.py:92
  456.4 9.8 custom-call.42
  468.4 11.9 %cholesky.343 = f32[128,128]{1,0:T(8,128)S(1)} custom-call(f32[128,128]{1,0:T(8,128)S(1)} %convolution_subtract_fusion.14), custom_call_target="Cholesky" | custom-call | tf_op jit(solution)/shard_map/jit(cholesky)/cholesky | solution.py:92
  485.0 2.4 select_select_fusion.1
  487.4 11.7 %while.15 = (s32[]{:T(128)}, f32[512,512]{1,0:T(8,128)}, s32[4,2]{0,1:T(2,128)S(1)}, f32[4,128,128]{2,1,0:T(8,128)S(1)}, s32[]{:T(128)}) while((s32[]{:T(128)}, f32[512,512]{1,0:T(8,128)}, s32[4,2]{0,1:T(2,128)S(1)}, f32[4,128,128]{2,1,0:T(8,128)S(1)}, s32[]{:T(128)}) %tuple.84), condition=%wide.while_cond.clone, body=%wide.while_body.clone.sunk | while | flops 2 | bytes 131189 | solution.py:44
  488.1 2.3 bitcast_dynamic-update-slice_fusion.4
  491.1 2.3 bitcast_dynamic-update-slice_fusion.4
  494.0 2.3 bitcast_dynamic-update-slice_fusion.4
  496.9 2.2 bitcast_dynamic-update-slice_fusion.4
  499.2 39.3 %custom-call.44 = f32[4,128,128]{1,2,0:T(8,128)S(1)} custom-call(f32[4,128,128]{2,1,0:T(8,128)S(1)} %get-tuple-element.64), custom_call_target="InvertDiagBlocksLowerTriangular" | custom-call | tf_op jit(solution)/shard_map/triangular_solve/custom-call.3 | solution.py:44
  562.8 12.1 %cholesky.358 = f32[128,128]{1,0:T(8,128)S(1)} custom-call(f32[128,128]{1,0:T(8,128)S(1)} %cholesky.439), custom_call_target="Cholesky" | custom-call | tf_op jit(solution)/shard_map/jit(cholesky)/cholesky | solution.py:99
  575.6 9.8 custom-call.45
  588.8 11.7 %cholesky.377 = f32[128,128]{1,0:T(8,128)S(1)} custom-call(f32[128,128]{1,0:T(8,128)S(1)} %cholesky.443), custom_call_target="Cholesky" | custom-call | tf_op jit(solution)/shard_map/jit(cholesky)/cholesky | solution.py:99
  601.2 9.8 custom-call.46
  613.5 11.9 %cholesky.398 = f32[128,128]{1,0:T(8,128)S(1)} custom-call(f32[128,128]{1,0:T(8,128)S(1)} %cholesky.448), custom_call_target="Cholesky" | custom-call | tf_op jit(solution)/shard_map/jit(cholesky)/cholesky | solution.py:99
  626.1 9.8 custom-call.47
  637.3 11.7 %cholesky.415 = f32[128,128]{1,0:T(8,128)S(1)} custom-call(f32[128,128]{1,0:T(8,128)S(1)} %convolution_subtract_fusion.13), custom_call_target="Cholesky" | custom-call | tf_op jit(solution)/shard_map/jit(cholesky)/cholesky | solution.py:99
  653.8 10.8 while.16
  665.4 40.3 %custom-call.50 = f32[4,128,128]{1,2,0:T(8,128)S(1)} custom-call(f32[4,128,128]{2,1,0:T(8,128)} %copy-done.26), custom_call_target="InvertDiagBlocksLowerTriangular" | custom-call | tf_op jit(solution)/shard_map/triangular_solve/custom-call.9 | solution.py:103
  712.3 9.4 all_gather.14
  721.7 5.5 collective-permute-start.5
  729.1 5.2 collective-permute-done.4
  735.1 2.4 gather_fusion.2
  737.5 3.6 multiply_reduce_fusion.3
  746.6 75.2 %all-reduce.1 = (f32[2,32]{1,0:T(2,128)}, f32[2,32]{1,0:T(2,128)}) all-reduce(f32[2,32]{1,0:T(2,128)} %dynamic_update_slice.22, f32[2,32]{1,0:T(2,128)} %dynamic_update_slice.21), channel_id=1, replica_groups=mesh['blk'=32,'leaf'=4,'samp'=2] {'blk','leaf','samp'}, use_global_device_ids=true, to_apply=%region_14.20 | all-reduce | flops 128 | bytes 1024 | tf_op jit(solution)/shard_map/psum | solution.py:79
  824.5 156.1 %all-reduce.6.cloned.1.call-done = f32[2,512,32]{1,2,0:T(8,128)} async-done(((f32[2,512,32]{1,2,0:T(8,128)}), f32[2,512,32]{1,2,0:T(8,128)}) %all-reduce.6.cloned.1.call-update) | async-done | bytes 131088 | tf_op jit(solution)/shard_map/psum | solution.py:79
  985.2 75.9 %psum.62 = f32[2,32]{1,0:T(2,128)S(1)} all-reduce(f32[2,32]{1,0:T(2,128)S(1)} %dynamic_update_slice.24), channel_id=1, replica_groups=mesh['blk'=32,'leaf'=4,'samp'=2] {'blk','leaf','samp'}, use_global_device_ids=true, to_apply=%region_17.23 | all-reduce | flops 64 | bytes 512 | tf_op jit(solution)/shard_map/psum | solution.py:79
  1062.0 9.1 all_gather.15
  1072.9 2.4 collective-permute-done.7
  1075.2 4.6 collective-permute-done.6
  1082.6 76.1 %psum.63 = f32[2,32]{1,0:T(2,128)S(1)} all-reduce(f32[2,32]{1,0:T(2,128)S(1)} %dynamic_update_slice.25), channel_id=1, replica_groups=mesh['blk'=32,'leaf'=4,'samp'=2] {'blk','leaf','samp'}, use_global_device_ids=true, to_apply=%region_19.25 | all-reduce | flops 64 | bytes 512 | tf_op jit(solution)/shard_map/psum | solution.py:79
  (260 shorter events, 106.3 us)
Async XLA Ops:
  7.2 39.9 %all-gather.2.cloned.1.call-start = ((), (), s32[]{:S(2)}) async-start(), calls=%async_computation | async-start | bytes 2621440 | tf_op jit(solution)/shard_map/all_gather | solution.py:39
  9.3 376.3 %all-reduce.8.cloned.1.call-start = ((), (), s32[]{:S(2)}) async-start(), calls=%async_computation.2 | async-start | bytes 4456448 | tf_op jit(solution)/shard_map/psum | solution.py:89
  19.8 34.3 %collective-permute-start.3 = (f32[3,1024]{1,0:T(4,128)S(1)}, f32[3,1024]{1,0:T(4,128)S(1)}, u32[]{:S(2)}, u32[]{:S(2)}) collective-permute-start(f32[3,1024]{1,0:T(4,128)S(1)} %all_gather.13), channel_id=1, source_target_pairs={{8,0},{16,8},{24,16},{32,24},{40,32},{48,40},{56,48},{64,56},{72,6... | collective-permute-start | bytes 36872 | tf_op jit(solution)/shard_map/ppermute | solution.py:17
  27.6 26.5 %collective-permute-start.2 = (f32[3,1024]{1,0:T(4,128)S(1)}, f32[3,1024]{1,0:T(4,128)S(1)}, u32[]{:S(2)}, u32[]{:S(2)}) collective-permute-start(f32[3,1024]{1,0:T(4,128)S(1)} %all_gather.13), channel_id=1, source_target_pairs={{248,0},{0,8},{8,16},{16,24},{24,32},{32,40},{40,48},{48,56},{56,6... | collective-permute-start | bytes 36872 | tf_op jit(solution)/shard_map/ppermute | solution.py:17
  47.1 49.8 %collective-permute-start.1 = (f32[512,1024]{0,1:T(8,128)}, f32[512,1024]{0,1:T(8,128)}, u32[]{:S(2)}, u32[]{:S(2)}) collective-permute-start(f32[512,1024]{0,1:T(8,128)} %all-gather.2.cloned.1.call-done), channel_id=1, source_target_pairs={{8,0},{16,8},{24,16},{32,24},{40,32},{48,40},{56,48},{64,56},{72,6... | collective-permute-start | bytes 6291464 | tf_op jit(solution)/shard_map/ppermute | solution.py:17
  52.2 49.8 %collective-permute-start = (f32[512,1024]{0,1:T(8,128)}, f32[512,1024]{0,1:T(8,128)}, u32[]{:S(2)}, u32[]{:S(2)}) collective-permute-start(f32[512,1024]{0,1:T(8,128)} %all-gather.2.cloned.1.call-done), channel_id=1, source_target_pairs={{248,0},{0,8},{8,16},{16,24},{24,32},{32,40},{40,48},{48,56},{56,6... | collective-permute-start | bytes 6291464 | tf_op jit(solution)/shard_map/ppermute | solution.py:17
  54.1 65.7 %copy-start.36 = (pred[8]{0:T(512)(128)(4,1)}, pred[8]{0:T(512)(128)(4,1)S(1)}, u32[]{:S(2)}) copy-start(pred[8]{0:T(512)(128)(4,1)S(1)} %compare_and_fusion) | copy-start | bytes 28
  56.0 46.0 %copy-start.11 = (f32[512,1024]{0,1:T(8,128)S(1)}, f32[512,1024]{0,1:T(8,128)}, u32[]{:S(2)}) copy-start(f32[512,1024]{0,1:T(8,128)} %all-gather.2.cloned.1.call-done) | copy-start | bytes 6291460
  114.2 5.6 copy-start.7
  125.2 4.0 copy-start
  125.2 4.0 copy-start.24
  125.2 4.0 copy-start.33
  130.5 850.0 %all-reduce.6.cloned.1.call-start = ((), (), s32[]{:S(2)}) async-start(), calls=%async_computation.1 | async-start | bytes 262144 | tf_op jit(solution)/shard_map/psum | solution.py:79
  393.5 1.0 copy-start.9
  441.1 1.0 copy-start.3
  443.3 95.2 %copy-start.1 = (f32[512,256]{1,0:T(8,128)S(1)}, f32[512,256]{1,0:T(8,128)}, u32[]{:S(2)}) copy-start(f32[512,256]{1,0:T(8,128)} %copy-done) | copy-start | bytes 1572868
  499.1 48.0 %copy-start.32 = (s32[4,2]{0,1:T(2,128)}, s32[4,2]{0,1:T(2,128)S(1)}, u32[]{:S(2)}) copy-start(s32[4,2]{0,1:T(2,128)S(1)} %get-tuple-element.250) | copy-start | bytes 100
  538.5 6.7 copy-start.2
  538.5 8.7 copy-start.15
  540.4 2.6 copy-start.23
  541.7 1.3 copy-start.25
  545.2 3.2 copy-start.12
  545.8 1.4 copy-start.20
  551.9 3.4 copy-start.5
  553.4 1.9 copy-start.6
  555.3 0.7 copy-start.10
  561.8 1.0 copy-start.8
  588.1 0.7 copy-start.16
  649.1 3.3 copy-start.4
  664.7 0.7 copy-start.26
  705.7 21.5 %copy-start.38 = (s32[8]{0:T(128)S(1)}, s32[8]{0:T(128)}, u32[]{:S(2)}) copy-start(s32[8]{0:T(128)} %get-tuple-element.93) | copy-start | bytes 100
  712.3 16.8 %copy-start.17 = (f32[32,256]{1,0:T(8,128)}, f32[32,256]{1,0:T(8,128)S(1)}, u32[]{:S(2)}) copy-start(f32[32,256]{1,0:T(8,128)S(1)} %convolution_subtract_fusion.16) | copy-start | bytes 98308
  721.7 7.5 collective-permute-start.5
  727.2 7.1 collective-permute-start.4
  737.5 4.3 copy-start.13
  737.5 4.3 copy-start.21
  737.5 4.3 copy-start.28
  980.6 4.1 copy-start.14
  980.6 4.1 copy-start.22
  980.6 4.1 copy-start.29
  980.6 4.1 copy-start.30
  981.6 79.5 %copy-start.39 = (f32[2,32]{1,0:T(2,128)S(1)}, f32[2,32]{1,0:T(2,128)}, u32[]{:S(2)}) copy-start(f32[2,32]{1,0:T(2,128)} %get-tuple-element.89) | copy-start | bytes 772
  983.5 97.0 %copy-start.37 = (pred[8]{0:T(512)(128)(4,1)S(1)}, pred[8]{0:T(512)(128)(4,1)}, u32[]{:S(2)}) copy-start(pred[8]{0:T(512)(128)(4,1)} %copy-done.36) | copy-start | bytes 28
  1071.1 87.7 %copy-start.18 = (f32[32,256]{1,0:T(8,128)S(1)}, f32[32,256]{1,0:T(8,128)}, u32[]{:S(2)}) copy-start(f32[32,256]{1,0:T(8,128)} %copy-done.17) | copy-start | bytes 98308
  1071.1 87.7 %copy-start.31 = (f32[32,256]{1,0:T(8,128)S(1)}, f32[32,256]{1,0:T(8,128)}, u32[]{:S(2)}) copy-start(f32[32,256]{1,0:T(8,128)} %multiply_subtract_fusion.1) | copy-start | bytes 98308
  1071.1 87.7 %copy-start.35 = (f32[32]{0:T(128)S(1)}, f32[32]{0:T(128)}, u32[]{:S(2)}) copy-start(f32[32]{0:T(128)} %copy-done.34) | copy-start | bytes 388
  1071.1 4.1 collective-permute-start.7
  1072.6 7.1 collective-permute-start.6
  (3 other events, 1.9 us)
Sparse Core Ops, SparseCore 0:
  9.8 37.2 all-gather.1
  130.7 254.8 all-reduce.7
  743.1 237.3 all-reduce.5
where the time goes:
time: 1180 us; the launch traced here: 1170 us
  waiting for transfers between devices  487 us (41%)
  other arithmetic  267 us (23%)
  blocking collectives  256 us (22%)
  local copies, waits for them, and re-layouts  59.4 us (5%)
  matrix products  55.7 us (5%)
  starting transfers between devices  20.6 us (2%)
  between operations  20.6 us (2%)
    psum x1, waiting for transfers between devices, local(): lax.psum((core_part, square_part, rhs_part), ALL_AXES)  255 us
    psum x3, blocking collectives, total_per_samp(): return jax.tree.map(unslot, lax.psum(jax.tree.map(slot, values), ALL_AXES))  227 us
    psum x1, waiting for transfers between devices, total_per_samp(): return jax.tree.map(unslot, lax.psum(jax.tree.map(slot, values), ALL_AXES))  156 us
    another operation x14, other arithmetic, local(): factor = jnp.linalg.cholesky(core_gram)  80.3 us
    another operation x15, other arithmetic, local(): wood_factor = jnp.linalg.cholesky(woodbury)  79.8 us
    ppermute x8, waiting for transfers between devices, shifted_2(): return lax.ppermute(block, axis, route)  56.8 us
    another operation x4, other arithmetic, lower_solve(): lax.linalg.triangular_solve(factor, values, left_side=True, lower=True)  41.8 us
    another operation x2, other arithmetic, precond_from(): lax.linalg.triangular_solve(wood_factor, first_solve, left_side=True, low...  41.7 us
  transfers between devices with their start and end apart: 11, of which 9 were waited for; matrix products, arithmetic and copies ran while one was open for 1% of the time, Pallas kernels for 0%

commit v1 on v0

--- a/solution.py
+++ b/solution.py
@@ -86,7 +86,9 @@
     core_part = high_dot(omega_half, sketch_half.T)
     square_part = high_dot(sketch_half, sketch_half.T)
     rhs_part = slot(high_dot(sketch, rhs.T))
-    core_gram, square_gram, rhs_proj = lax.psum((core_part, square_part, rhs_part), ALL_AXES)
+    core_gram, square_gram, rhs_proj = lax.psum(
+        lax.psum((core_part, square_part, rhs_part), ("leaf", "samp")), "blk"
+    )
     rhs_proj = unslot(rhs_proj)
     core_gram = 0.5 * (core_gram + core_gram.T)
     factor = jnp.linalg.cholesky(core_gram)

time: 1180 us -> 1150 us (0.975)
  waiting for transfers between devices: 487 us -> 451 us
    psum x1 -> x2, waiting for transfers between devices: 255 us -> 220 us  [the longest x1 156 us: local(): lax.psum(lax.psum((core_part, square_part, rhs_part), ('leaf', 'samp')),...]
  transfers between devices with their start and end apart: 11 -> 12, of which waited for: 9 -> 10; matrix products, arithmetic and copies ran while one was open for 1% -> 1% of each run, Pallas kernels for 0% -> 0%
where the time goes in v1:
time: 1150 us; the launch traced here: 1140 us
  waiting for transfers between devices  451 us (39%)
  other arithmetic  267 us (23%)
  blocking collectives  263 us (23%)
  local copies, waits for them, and re-layouts  60 us (5%)
  matrix products  55.7 us (5%)
  between operations  20.5 us (2%)
  starting transfers between devices  18.1 us (2%)
    psum x3, blocking collectives, total_per_samp(): return jax.tree.map(unslot, lax.psum(jax.tree.map(slot, values), ALL_AXES))  234 us
    psum x1, waiting for transfers between devices, local(): lax.psum(lax.psum((core_part, square_part, rhs_part), ('leaf', 'samp')),...  156 us
    psum x1, waiting for transfers between devices, total_per_samp(): return jax.tree.map(unslot, lax.psum(jax.tree.map(slot, values), ALL_AXES))  155 us
    another operation x14, other arithmetic, local(): factor = jnp.linalg.cholesky(core_gram)  80.4 us
    another operation x15, other arithmetic, local(): wood_factor = jnp.linalg.cholesky(woodbury)  79.8 us
    psum x1, waiting for transfers between devices, local(): lax.psum((core_part, square_part, rhs_part), ('leaf', 'samp'))  63.9 us
    ppermute x8, waiting for transfers between devices, shifted_2(): return lax.ppermute(block, axis, route)  56.8 us
    another operation x4, other arithmetic, lower_solve(): lax.linalg.triangular_solve(factor, values, left_side=True, lower=True)  41.8 us
  transfers between devices with their start and end apart: 12, of which 10 were waited for; matrix products, arithmetic and copies ran while one was open for 1% of the time, Pallas kernels for 0%

profile of v1, /device:TPU:1, one launch (start us, length us, event | category | flops | bytes accessed | tf_op | source)
XLA Modules:
  0.0 1135.4 jit_solution(16777836520307094748)
XLA Ops:
  9.3 10.5 all_gather.13
  19.9 7.8 collective-permute-start.3
  27.6 19.4 %all-gather.2.cloned.1.call-done = f32[512,1024]{0,1:T(8,128)} async-done(((f32[512,256]{0,1:T(8,128)}), f32[512,1024]{0,1:T(8,128)}) %all-gather.2.cloned.1.call-update) | async-done | bytes 2097168 | tf_op jit(solution)/shard_map/all_gather | solution.py:39
  47.1 5.2 collective-permute-start.1
  56.0 2.6 multiply_multiply_fusion
  58.7 38.2 %collective-permute-done.1 = f32[512,1024]{0,1:T(8,128)} collective-permute-done((f32[512,1024]{0,1:T(8,128)}, f32[512,1024]{0,1:T(8,128)}, u32[]{:S(2)}, u32[]{:S(2)}) %collective-permute-start.1) | collective-permute-done | bytes 2097184 | tf_op jit(solution)/shard_map/ppermute | solution.py:17
  96.8 5.2 collective-permute-done
  102.0 5.6 pad_maximum_fusion
  107.6 6.5 copy.12
  114.2 5.6 gather_fusion
  119.8 5.5 fusion.17
  130.6 63.9 %all-reduce.12.cloned.1.call-done = (f32[512,512]{1,0:T(8,128)}, f32[2,512,32]{1,2,0:T(8,128)}, f32[512,512]{1,0:T(8,128)}) async-done(((f32[512,512]{1,0:T(8,128)}, f32[2,512,32]{1,2,0:T(8,128)}, f32[512,512]{1,0:T(8,128)}), (f32[512,512]{1,0:T(8,128)}, f32[2,512,32]{1,2,0:T(8,128)}, f32[512,512]{1,0:T(8,128)})) %all-reduce.12.cloned.1.call-update) | async-done | bytes 2228240 | tf_op jit(solution)/shard_map/psum | solution.py:90
  194.8 156.1 %all-reduce.10.cloned.1.call-done = (f32[512,512]{1,0:T(8,128)}, f32[2,512,32]{1,2,0:T(8,128)}, f32[512,512]{1,0:T(8,128)}) async-done(((f32[512,512]{1,0:T(8,128)}, f32[2,512,32]{1,2,0:T(8,128)}, f32[512,512]{1,0:T(8,128)}), (f32[512,512]{1,0:T(8,128)}, f32[2,512,32]{1,2,0:T(8,128)}, f32[512,512]{1,0:T(8,128)})) %all-reduce.10.cloned.1.call-update) | async-done | bytes 2228240 | tf_op jit(solution)/shard_map/psum | solution.py:89
  351.7 2.6 copy.14
  360.0 11.7 %cholesky.286 = f32[128,128]{1,0:T(8,128)S(1)} custom-call(f32[128,128]{1,0:T(8,128)S(1)} %cholesky.426), custom_call_target="Cholesky" | custom-call | tf_op jit(solution)/shard_map/jit(cholesky)/cholesky | solution.py:94
  371.7 9.8 custom-call.40
  384.2 11.7 %cholesky.305 = f32[128,128]{1,0:T(8,128)S(1)} custom-call(f32[128,128]{1,0:T(8,128)S(1)} %cholesky.430), custom_call_target="Cholesky" | custom-call | tf_op jit(solution)/shard_map/jit(cholesky)/cholesky | solution.py:94
  395.9 10.3 custom-call.41
  408.7 11.7 %cholesky.326 = f32[128,128]{1,0:T(8,128)S(1)} custom-call(f32[128,128]{1,0:T(8,128)S(1)} %cholesky.435), custom_call_target="Cholesky" | custom-call | tf_op jit(solution)/shard_map/jit(cholesky)/cholesky | solution.py:94
  421.8 9.8 custom-call.42
  433.9 11.9 %cholesky.343 = f32[128,128]{1,0:T(8,128)S(1)} custom-call(f32[128,128]{1,0:T(8,128)S(1)} %convolution_subtract_fusion.14), custom_call_target="Cholesky" | custom-call | tf_op jit(solution)/shard_map/jit(cholesky)/cholesky | solution.py:94
  450.4 2.4 select_select_fusion.1
  452.8 12.2 %while.15 = (s32[]{:T(128)}, f32[512,512]{1,0:T(8,128)}, s32[4,2]{0,1:T(2,128)S(1)}, f32[4,128,128]{2,1,0:T(8,128)S(1)}, s32[]{:T(128)}) while((s32[]{:T(128)}, f32[512,512]{1,0:T(8,128)}, s32[4,2]{0,1:T(2,128)S(1)}, f32[4,128,128]{2,1,0:T(8,128)S(1)}, s32[]{:T(128)}) %tuple.84), condition=%wide.while_cond.clone, body=%wide.while_body.clone.sunk | while | flops 2 | bytes 131189 | solution.py:44
  453.5 2.4 bitcast_dynamic-update-slice_fusion.4
  456.6 2.4 bitcast_dynamic-update-slice_fusion.4
  459.6 2.4 bitcast_dynamic-update-slice_fusion.4
  465.0 39.3 %custom-call.44 = f32[4,128,128]{1,2,0:T(8,128)S(1)} custom-call(f32[4,128,128]{2,1,0:T(8,128)S(1)} %get-tuple-element.64), custom_call_target="InvertDiagBlocksLowerTriangular" | custom-call | tf_op jit(solution)/shard_map/triangular_solve/custom-call.3 | solution.py:44
  528.6 12.1 %cholesky.358 = f32[128,128]{1,0:T(8,128)S(1)} custom-call(f32[128,128]{1,0:T(8,128)S(1)} %cholesky.439), custom_call_target="Cholesky" | custom-call | tf_op jit(solution)/shard_map/jit(cholesky)/cholesky | solution.py:101
  541.4 9.8 custom-call.45
  554.6 11.7 %cholesky.377 = f32[128,128]{1,0:T(8,128)S(1)} custom-call(f32[128,128]{1,0:T(8,128)S(1)} %cholesky.443), custom_call_target="Cholesky" | custom-call | tf_op jit(solution)/shard_map/jit(cholesky)/cholesky | solution.py:101
  567.0 9.8 custom-call.46
  579.3 11.9 %cholesky.398 = f32[128,128]{1,0:T(8,128)S(1)} custom-call(f32[128,128]{1,0:T(8,128)S(1)} %cholesky.448), custom_call_target="Cholesky" | custom-call | tf_op jit(solution)/shard_map/jit(cholesky)/cholesky | solution.py:101
  591.9 9.8 custom-call.47
  603.2 11.7 %cholesky.415 = f32[128,128]{1,0:T(8,128)S(1)} custom-call(f32[128,128]{1,0:T(8,128)S(1)} %convolution_subtract_fusion.13), custom_call_target="Cholesky" | custom-call | tf_op jit(solution)/shard_map/jit(cholesky)/cholesky | solution.py:101
  619.6 10.8 while.16
  631.0 40.3 %custom-call.50 = f32[4,128,128]{1,2,0:T(8,128)S(1)} custom-call(f32[4,128,128]{2,1,0:T(8,128)} %copy-done.26), custom_call_target="InvertDiagBlocksLowerTriangular" | custom-call | tf_op jit(solution)/shard_map/triangular_solve/custom-call.9 | solution.py:105
  678.0 9.4 all_gather.14
  687.4 3.0 collective-permute-start.5
  692.4 5.2 collective-permute-done.4
  698.4 2.4 gather_fusion.2
  700.7 3.6 multiply_reduce_fusion.3
  710.0 82.1 %all-reduce.1 = (f32[2,32]{1,0:T(2,128)}, f32[2,32]{1,0:T(2,128)}) all-reduce(f32[2,32]{1,0:T(2,128)} %dynamic_update_slice.22, f32[2,32]{1,0:T(2,128)} %dynamic_update_slice.21), channel_id=1, replica_groups=mesh['blk'=32,'leaf'=4,'samp'=2] {'blk','leaf','samp'}, use_global_device_ids=true, to_apply=%region_17.23 | all-reduce | flops 128 | bytes 1024 | tf_op jit(solution)/shard_map/psum | solution.py:79
  794.8 154.8 %all-reduce.8.cloned.1.call-done = f32[2,512,32]{1,2,0:T(8,128)} async-done(((f32[2,512,32]{1,2,0:T(8,128)}), f32[2,512,32]{1,2,0:T(8,128)}) %all-reduce.8.cloned.1.call-update) | async-done | bytes 131088 | tf_op jit(solution)/shard_map/psum | solution.py:79
  954.2 75.9 %psum.86 = f32[2,32]{1,0:T(2,128)S(1)} all-reduce(f32[2,32]{1,0:T(2,128)S(1)} %dynamic_update_slice.24), channel_id=1, replica_groups=mesh['blk'=32,'leaf'=4,'samp'=2] {'blk','leaf','samp'}, use_global_device_ids=true, to_apply=%region_20.26 | all-reduce | flops 64 | bytes 512 | tf_op jit(solution)/shard_map/psum | solution.py:79
  1030.9 9.1 all_gather.15
  1041.8 2.4 collective-permute-done.7
  1044.2 4.6 collective-permute-done.6
  1051.6 76.1 %psum.87 = f32[2,32]{1,0:T(2,128)S(1)} all-reduce(f32[2,32]{1,0:T(2,128)S(1)} %dynamic_update_slice.25), channel_id=1, replica_groups=mesh['blk'=32,'leaf'=4,'samp'=2] {'blk','leaf','samp'}, use_global_device_ids=true, to_apply=%region_22.28 | all-reduce | flops 64 | bytes 512 | tf_op jit(solution)/shard_map/psum | solution.py:79
  (263 shorter events, 108.7 us)
Async XLA Ops:
  7.2 39.9 %all-gather.2.cloned.1.call-start = ((), (), s32[]{:S(2)}) async-start(), calls=%async_computation | async-start | bytes 2621440 | tf_op jit(solution)/shard_map/all_gather | solution.py:39
  9.3 185.2 %all-reduce.12.cloned.1.call-start = ((), (), s32[]{:S(2)}) async-start(), calls=%async_computation.3 | async-start | bytes 4456448 | tf_op jit(solution)/shard_map/psum | solution.py:90
  19.9 34.3 %collective-permute-start.3 = (f32[3,1024]{1,0:T(4,128)S(1)}, f32[3,1024]{1,0:T(4,128)S(1)}, u32[]{:S(2)}, u32[]{:S(2)}) collective-permute-start(f32[3,1024]{1,0:T(4,128)S(1)} %all_gather.13), channel_id=1, source_target_pairs={{8,0},{16,8},{24,16},{32,24},{40,32},{48,40},{56,48},{64,56},{72,6... | collective-permute-start | bytes 36872 | tf_op jit(solution)/shard_map/ppermute | solution.py:17
  27.6 26.5 %collective-permute-start.2 = (f32[3,1024]{1,0:T(4,128)S(1)}, f32[3,1024]{1,0:T(4,128)S(1)}, u32[]{:S(2)}, u32[]{:S(2)}) collective-permute-start(f32[3,1024]{1,0:T(4,128)S(1)} %all_gather.13), channel_id=1, source_target_pairs={{248,0},{0,8},{8,16},{16,24},{24,32},{32,40},{40,48},{48,56},{56,6... | collective-permute-start | bytes 36872 | tf_op jit(solution)/shard_map/ppermute | solution.py:17
  47.1 49.8 %collective-permute-start.1 = (f32[512,1024]{0,1:T(8,128)}, f32[512,1024]{0,1:T(8,128)}, u32[]{:S(2)}, u32[]{:S(2)}) collective-permute-start(f32[512,1024]{0,1:T(8,128)} %all-gather.2.cloned.1.call-done), channel_id=1, source_target_pairs={{8,0},{16,8},{24,16},{32,24},{40,32},{48,40},{56,48},{64,56},{72,6... | collective-permute-start | bytes 6291464 | tf_op jit(solution)/shard_map/ppermute | solution.py:17
  52.2 49.8 %collective-permute-start = (f32[512,1024]{0,1:T(8,128)}, f32[512,1024]{0,1:T(8,128)}, u32[]{:S(2)}, u32[]{:S(2)}) collective-permute-start(f32[512,1024]{0,1:T(8,128)} %all-gather.2.cloned.1.call-done), channel_id=1, source_target_pairs={{248,0},{0,8},{8,16},{16,24},{24,32},{32,40},{40,48},{48,56},{56,6... | collective-permute-start | bytes 6291464 | tf_op jit(solution)/shard_map/ppermute | solution.py:17
  54.1 65.7 %copy-start.36 = (pred[8]{0:T(512)(128)(4,1)}, pred[8]{0:T(512)(128)(4,1)S(1)}, u32[]{:S(2)}) copy-start(pred[8]{0:T(512)(128)(4,1)S(1)} %compare_and_fusion) | copy-start | bytes 28
  56.0 46.0 %copy-start.11 = (f32[512,1024]{0,1:T(8,128)S(1)}, f32[512,1024]{0,1:T(8,128)}, u32[]{:S(2)}) copy-start(f32[512,1024]{0,1:T(8,128)} %all-gather.2.cloned.1.call-done) | copy-start | bytes 6291460
  114.2 5.6 copy-start.7
  125.2 4.0 copy-start
  125.3 4.0 copy-start.24
  125.3 4.0 copy-start.33
  130.6 220.3 %all-reduce.10.cloned.1.call-start = ((), (), s32[]{:S(2)}) async-start(), calls=%async_computation.2 | async-start | bytes 4456448 | tf_op jit(solution)/shard_map/psum | solution.py:89
  194.5 755.1 %all-reduce.8.cloned.1.call-start = ((), (), s32[]{:S(2)}) async-start(), calls=%async_computation.1 | async-start | bytes 262144 | tf_op jit(solution)/shard_map/psum | solution.py:79
  358.9 1.0 copy-start.9
  406.4 1.0 copy-start.3
  408.7 95.6 %copy-start.1 = (f32[512,256]{1,0:T(8,128)S(1)}, f32[512,256]{1,0:T(8,128)}, u32[]{:S(2)}) copy-start(f32[512,256]{1,0:T(8,128)} %copy-done) | copy-start | bytes 1572868
  465.0 48.0 %copy-start.32 = (s32[4,2]{0,1:T(2,128)}, s32[4,2]{0,1:T(2,128)S(1)}, u32[]{:S(2)}) copy-start(s32[4,2]{0,1:T(2,128)S(1)} %get-tuple-element.267) | copy-start | bytes 100
  504.4 6.7 copy-start.2
  504.4 8.7 copy-start.15
  506.2 2.6 copy-start.23
  507.6 1.3 copy-start.25
  511.1 3.2 copy-start.12
  511.7 1.4 copy-start.20
  517.8 3.4 copy-start.5
  519.2 1.9 copy-start.6
  521.2 0.7 copy-start.10
  527.6 1.0 copy-start.8
  614.9 3.3 copy-start.4
  630.3 0.7 copy-start.26
  671.4 19.0 %copy-start.38 = (s32[8]{0:T(128)S(1)}, s32[8]{0:T(128)}, u32[]{:S(2)}) copy-start(s32[8]{0:T(128)} %get-tuple-element.96) | copy-start | bytes 100
  678.0 14.4 %copy-start.17 = (f32[32,256]{1,0:T(8,128)}, f32[32,256]{1,0:T(8,128)S(1)}, u32[]{:S(2)}) copy-start(f32[32,256]{1,0:T(8,128)S(1)} %convolution_subtract_fusion.16) | copy-start | bytes 98308
  687.4 4.9 collective-permute-start.5
  690.4 7.1 collective-permute-start.4
  700.7 4.3 copy-start.13
  700.7 4.3 copy-start.21
  700.7 4.3 copy-start.28
  949.6 4.1 copy-start.14
  949.6 4.1 copy-start.22
  949.6 4.1 copy-start.29
  949.6 4.1 copy-start.30
  950.6 79.5 %copy-start.39 = (f32[2,32]{1,0:T(2,128)S(1)}, f32[2,32]{1,0:T(2,128)}, u32[]{:S(2)}) copy-start(f32[2,32]{1,0:T(2,128)} %get-tuple-element.89) | copy-start | bytes 772
  952.5 97.0 %copy-start.37 = (pred[8]{0:T(512)(128)(4,1)S(1)}, pred[8]{0:T(512)(128)(4,1)}, u32[]{:S(2)}) copy-start(pred[8]{0:T(512)(128)(4,1)} %copy-done.36) | copy-start | bytes 28
  1040.0 87.7 %copy-start.18 = (f32[32,256]{1,0:T(8,128)S(1)}, f32[32,256]{1,0:T(8,128)}, u32[]{:S(2)}) copy-start(f32[32,256]{1,0:T(8,128)} %copy-done.17) | copy-start | bytes 98308
  1040.0 87.7 %copy-start.31 = (f32[32,256]{1,0:T(8,128)S(1)}, f32[32,256]{1,0:T(8,128)}, u32[]{:S(2)}) copy-start(f32[32,256]{1,0:T(8,128)} %multiply_subtract_fusion.1) | copy-start | bytes 98308
  1040.0 87.7 %copy-start.35 = (f32[32]{0:T(128)S(1)}, f32[32]{0:T(128)}, u32[]{:S(2)}) copy-start(f32[32]{0:T(128)} %copy-done.34) | copy-start | bytes 388
  1040.0 4.1 collective-permute-start.7
  1041.6 7.1 collective-permute-start.6
  (4 other events, 2.5 us)
Sparse Core Ops, SparseCore 0:
  9.8 37.2 all-gather.1
  130.7 63.7 all-reduce.11
  198.8 152.0 all-reduce.9
  706.4 243.0 all-reduce.7
